TPU v7x, 512 devices: a whole 4x8x8 slice. The times are simulated.
512 devices in a mesh: wide: 64 (over y, z), narrow: 8 (over x, core).
Axes of the slice: x: 4, y: 8, z: 8, core: 2. Of those that a mesh axis runs over, the one named last changes fastest.
Arguments:
- hidden: bfloat16 [16384, 1536], P('wide', 'narrow'), may hold values from -6 to 6
- start_state: bfloat16 [1024, 24, 64, 128], P('wide', 'narrow'), may hold values from -0.59765625 to 0.59765625
- tail_inner: bfloat16 [1024, 3, 1536], P('wide', None, 'narrow'), may hold values from -6 to 6
- tail_shared: bfloat16 [1024, 3, 256], P('wide'), may hold values from -6 to 6
- input_gain: float32 [1536], replicated, may hold values from 0.5 to 1.5
- w_gate_inner: bfloat16 [1536, 3072], P(None, 'narrow'), may hold values from -0.15625 to 0.15625
- w_shared: bfloat16 [1536, 256], P(None, 'narrow'), may hold values from -0.15625 to 0.15625
- w_step: bfloat16 [1536, 24], P(None, 'narrow'), may hold values from -0.15625 to 0.15625
- step_bias: float32 [24], P('narrow'), may hold values from -4 to -1
- decay_log: float32 [24], P('narrow'), may hold values from 0 to 2.5
- conv_inner: bfloat16 [4, 1536], P(None, 'narrow'), may hold values from -3 to 3
- conv_inner_bias: float32 [1536], P('narrow'), may hold values from -1.5 to 1.5
- conv_shared: bfloat16 [4, 256], replicated, may hold values from -3 to 3
- conv_shared_bias: float32 [256], replicated, may hold values from -1.5 to 1.5
- skip_gain: float32 [24], P('narrow'), may hold values from 0.5 to 1.5
- gated_gain: float32 [1536], P('narrow'), may hold values from 0.5 to 1.5
- w_output: bfloat16 [1536, 1536], P('narrow'), may hold values from -0.15625 to 0.15625
- next_gain: float32 [1536], replicated, may hold values from 0.5 to 1.5
- w_next: bfloat16 [1536, 3224], P(None, 'narrow'), may hold values from -0.15625 to 0.15625
- dealing: int32 [1024], replicated, may hold values from 0 to 1023, as said below
- accepted: int32 [1024], replicated, may hold values from 0 to 16
- owners: int32 [1024], replicated, may hold values from 0 to 63, as said below
Outputs:
- new_hidden: bfloat16 [16384, 1536], P('wide', 'narrow')
- next_input: bfloat16 [16384, 3224], P('wide', 'narrow')
- kept_state: bfloat16 [1024, 24, 64, 128], P('wide', 'narrow')
- kept_tail_inner: bfloat16 [1024, 3, 1536], P('wide', None, 'narrow')
- kept_tail_shared: bfloat16 [1024, 3, 256], P('wide')
Inputs may be any that keep to these rules, and one draw needn't show every extreme that they name: `dealing`: a permutation of the 1024 requests; slot j lies on index j // 16 of wide. Each owner keeps exactly 16 requests, and the requests of the slots of one index of wide have different owners.
All inputs are finite; a program needn't handle non-finite values.
Results may differ from a plain program's by a relative error of at most 0.02.
Values may be sent and summed in bfloat16 or wider, within the bound.
A program may use at most 64 MiB of HBM per device.

v0:
```python
import jax
import jax.numpy as jnp
from jax import lax
from jax.sharding import PartitionSpec as P

EPSILON = 1e-05
HIGHEST = lax.Precision.HIGHEST


def root_norm(values, gain):
    values = values.astype(jnp.float32)
    factor = lax.rsqrt(jnp.mean(values * values, axis=-1, keepdims=True) + EPSILON)
    return (values * factor * gain).astype(jnp.bfloat16)


def causal_filter(tail, fresh, weight, offset):
    extended = jnp.concatenate([tail, fresh], axis=1)
    length = fresh.shape[1]
    summed = jnp.zeros(fresh.shape, jnp.float32) + offset
    for place in range(weight.shape[0]):
        summed = summed + extended[:, place : place + length].astype(jnp.float32) * weight[
            place
        ].astype(jnp.float32)
    return (jax.nn.silu(summed), extended)


def pick_rows(extended, accepted_now, count):
    length = extended.shape[1]
    wanted = accepted_now[:, None] + jnp.arange(count, dtype=jnp.int32)[None, :]
    onehot = (wanted[:, :, None] == jnp.arange(length, dtype=jnp.int32)[None, None, :]).astype(
        jnp.float32
    )
    return jnp.einsum(
        "rqe,rec->rqc", onehot, extended.astype(jnp.float32), precision=HIGHEST
    ).astype(jnp.bfloat16)


def state_block(
    inner, shared, step_raw, step_bias, decay_log, skip_gain, start_state, accepted_now
):
    states = shared.shape[-1] // 2
    b_part = shared[..., :states]
    c_part = shared[..., states:]
    length = inner.shape[1]
    steps_now = jax.nn.softplus(step_raw.astype(jnp.float32) + step_bias)
    log_decay = steps_now * -jnp.exp(decay_log)
    cumul = jnp.cumsum(log_decay, axis=1)
    prefix = jnp.concatenate([jnp.zeros_like(cumul[:, :1]), cumul], axis=1)
    places = jnp.arange(length, dtype=jnp.int32)
    lower = (places[:, None] >= places[None, :])[None, :, :, None]
    spread = cumul[:, :, None, :] - cumul[:, None, :, :]
    weights = (
        jnp.where(lower, jnp.exp(jnp.where(lower, spread, 0.0)), 0.0) * steps_now[:, None, :, :]
    )
    intersection = jnp.einsum("rtn,rsn->rts", c_part, b_part, precision=HIGHEST)
    mixing = weights * intersection[:, :, :, None]
    state_now = start_state.astype(jnp.float32)
    carried = (
        jnp.einsum("rtn,rhpn->rthp", c_part, state_now, precision=HIGHEST)
        * jnp.exp(cumul)[:, :, :, None]
    )
    direct = jnp.einsum("rtsh,rshp->rthp", mixing, inner, precision=HIGHEST)
    outputs = carried + direct + skip_gain[:, None] * inner
    chosen = (jnp.arange(length + 1, dtype=jnp.int32)[None, :] == accepted_now[:, None]).astype(
        jnp.float32
    )
    ending = jnp.einsum("rk,rkh->rh", chosen, prefix, precision=HIGHEST)
    before = (places[None, :] < accepted_now[:, None])[:, :, None]
    factor = (
        jnp.where(before, jnp.exp(jnp.where(before, ending[:, None, :] - cumul, 0.0)), 0.0)
        * steps_now
    )
    kept = jnp.exp(ending)[:, :, None, None] * state_now + jnp.einsum(
        "rsh,rshp,rsn->rhpn", factor, inner, b_part, precision=HIGHEST
    )
    return (outputs, kept.astype(jnp.bfloat16))


def local(
    hidden,
    start_state,
    tail_inner,
    tail_shared,
    input_gain,
    w_gate_inner,
    w_shared,
    w_step,
    step_bias,
    decay_log,
    conv_inner,
    conv_inner_bias,
    conv_shared,
    conv_shared_bias,
    skip_gain,
    gated_gain,
    w_output,
    next_gain,
    w_next,
    dealing,
    accepted,
    owners,
):
    wide_index = lax.axis_index("wide")
    wide_count = lax.axis_size("wide")
    narrow_count = lax.axis_size("narrow")
    full_rows = lax.all_gather(hidden, "narrow", axis=1, tiled=True)
    normed_in = root_norm(full_rows, input_gain)
    tokens = full_rows.shape[0]
    requests = start_state.shape[0]
    length = tokens // requests
    heads_here = w_step.shape[1]
    head_size = start_state.shape[2]
    block = w_output.shape[0]
    gate_inner = jnp.dot(normed_in, w_gate_inner, preferred_element_type=jnp.float32).astype(
        jnp.bfloat16
    )
    shared_piece = jnp.dot(normed_in, w_shared, preferred_element_type=jnp.float32).astype(
        jnp.bfloat16
    )
    step_raw = jnp.dot(normed_in, w_step, preferred_element_type=jnp.float32).astype(jnp.bfloat16)
    shared_in = lax.all_gather(shared_piece, "narrow", axis=1, tiled=True)
    gate_part = gate_inner[:, :block]
    inner_in = gate_inner[:, block:]
    inner_conv, inner_ext = causal_filter(
        tail_inner, inner_in.reshape(requests, length, block), conv_inner, conv_inner_bias
    )
    shared_conv, shared_ext = causal_filter(
        tail_shared, shared_in.reshape(requests, length, -1), conv_shared, conv_shared_bias
    )
    first_slot = wide_index * requests
    slot_requests = lax.dynamic_slice_in_dim(dealing, first_slot, requests)
    accepted_now = jnp.take(accepted, slot_requests)
    outputs, kept = state_block(
        inner_conv.reshape(requests, length, heads_here, head_size),
        shared_conv,
        step_raw.reshape(requests, length, heads_here),
        step_bias,
        decay_log,
        skip_gain,
        start_state,
        accepted_now,
    )
    gated = outputs.reshape(tokens, block) * jax.nn.silu(gate_part.astype(jnp.float32))
    squares = lax.psum(jnp.sum(gated * gated, axis=1, keepdims=True), "narrow")
    gated_norm = (
        gated * lax.rsqrt(squares / (block * narrow_count) + EPSILON) * gated_gain
    ).astype(jnp.bfloat16)
    partial_sum = jnp.dot(gated_norm, w_output, preferred_element_type=jnp.float32)
    whole_sum = lax.psum(partial_sum.astype(jnp.bfloat16), "narrow").astype(jnp.float32)
    new_full = (full_rows.astype(jnp.float32) + whole_sum).astype(jnp.bfloat16)
    new_part = lax.dynamic_slice_in_dim(
        new_full, lax.axis_index("narrow") * hidden.shape[1], hidden.shape[1], 1
    )
    normed_next = root_norm(new_full, next_gain)
    next_input = jnp.dot(normed_next, w_next, preferred_element_type=jnp.float32).astype(
        jnp.bfloat16
    )
    owner_table = (owners[:, None] == jnp.arange(wide_count, dtype=jnp.int32)[None, :]).astype(
        jnp.int32
    )
    ranking = jnp.sum((jnp.cumsum(owner_table, axis=0) - owner_table) * owner_table, axis=1)
    slot_owner = jnp.take(owners, dealing)
    slot_rank = jnp.take(ranking, dealing)
    local_owner = lax.dynamic_slice_in_dim(slot_owner, first_slot, requests)
    send_table = (jnp.arange(wide_count, dtype=jnp.int32)[:, None] == local_owner[None, :]).astype(
        jnp.bfloat16
    )
    state_bucket = (
        jnp.dot(send_table, kept.reshape(requests, -1), preferred_element_type=jnp.float32)
        .astype(jnp.bfloat16)
        .reshape((wide_count,) + kept.shape[1:])
    )
    inner_edge = pick_rows(inner_ext, accepted_now, tail_inner.shape[1])
    shared_edge = pick_rows(shared_ext, accepted_now, tail_shared.shape[1])
    inner_bucket = jnp.einsum(
        "or,rqc->oqc", send_table, inner_edge, preferred_element_type=jnp.float32
    ).astype(jnp.bfloat16)
    shared_bucket = jnp.einsum(
        "or,rqc->oqc", send_table, shared_edge, preferred_element_type=jnp.float32
    ).astype(jnp.bfloat16)
    state_recv, inner_recv, shared_recv = (
        lax.all_to_all(state_bucket, "wide", split_axis=0, concat_axis=0, tiled=True),
        lax.all_to_all(inner_bucket, "wide", split_axis=0, concat_axis=0, tiled=True),
        lax.all_to_all(shared_bucket, "wide", split_axis=0, concat_axis=0, tiled=True),
    )
    senders = jnp.arange(slot_owner.shape[0], dtype=jnp.int32) // requests
    mine = slot_owner == wide_index
    picking = (
        (slot_rank[:, None] == jnp.arange(requests, dtype=jnp.int32)[None, :]) & mine[:, None]
    ).astype(jnp.bfloat16)
    from_sender = (senders[:, None] == jnp.arange(wide_count, dtype=jnp.int32)[None, :]).astype(
        jnp.bfloat16
    )
    selector = jnp.einsum(
        "jk,jw->kw", picking, from_sender, preferred_element_type=jnp.float32
    ).astype(jnp.bfloat16)
    kept_state = (
        jnp.dot(selector, state_recv.reshape(wide_count, -1), preferred_element_type=jnp.float32)
        .astype(jnp.bfloat16)
        .reshape(start_state.shape)
    )
    kept_tail_inner = jnp.einsum(
        "kw,wqc->kqc", selector, inner_recv, preferred_element_type=jnp.float32
    ).astype(jnp.bfloat16)
    kept_tail_shared = jnp.einsum(
        "kw,wqc->kqc", selector, shared_recv, preferred_element_type=jnp.float32
    ).astype(jnp.bfloat16)
    return (new_part, next_input, kept_state, kept_tail_inner, kept_tail_shared)


def solution(mesh):
    placed = (
        P("wide", "narrow"),
        P("wide", "narrow", None, None),
        P("wide", None, "narrow"),
        P("wide", None, None),
        P(),
        P(None, "narrow"),
        P(None, "narrow"),
        P(None, "narrow"),
        P("narrow"),
        P("narrow"),
        P(None, "narrow"),
        P("narrow"),
        P(),
        P(),
        P("narrow"),
        P("narrow"),
        P("narrow", None),
        P(),
        P(None, "narrow"),
        P(),
        P(),
        P(),
    )
    return jax.shard_map(
        local,
        mesh=mesh,
        in_specs=placed,
        out_specs=(
            P("wide", "narrow"),
            P("wide", "narrow"),
            P("wide", "narrow", None, None),
            P("wide", None, "narrow"),
            P("wide", None, None),
        ),
        check_vma=False,
    )
```

profile of v0, /device:TPU:24, one launch (start us, length us, event | category | flops | bytes accessed | tf_op | source)
XLA Modules:
  0.0 219.7 jit_solution(16669502044702229559)
XLA Ops:
  8.8 1.3 gather_fusion
  10.9 4.5 %gather_fusion.2 = s32[1024]{0:T(1024)S(1)} fusion(s32[1024]{0:T(1024)S(1)} %copy-done.1, s32[1024]{0:T(1024)S(1)} %fusion.81), kind=kCustom, calls=%fused_computation.1.clone | custom fusion | bytes 12288 | tf_op jit(solution)/shard_map/jit(_take)/gather | solution.py:162
  16.2 13.7 %all_gather.6 = bf16[256,1536]{0,1:T(8,128)(2,1)S(1)} all-gather(bf16[256,192]{0,1:T(8,128)(2,1)S(1)} %copy-done.7), channel_id=1, replica_groups=mesh['wide'=64,'narrow'=8] {'narrow'}, dimensions={1}, use_global_device_ids=true | all-gather | bytes 884736 | tf_op jit(solution)/shard_map/all_gather | solution.py:106
  30.5 1.9 convolution_convert_fusion.4
  34.4 16.6 %all-to-all-start.1 = ((bf16[64,3,192]{2,1,0:T(4,128)(2,1)}), bf16[64,3,192]{2,1,0:T(4,128)(2,1)}, u32[]{:S(2)}, u32[]{:S(2)}) async-start(bf16[64,3,192]{2,1,0:T(4,128)(2,1)} %copy.98), calls=%async_computation.1 | async-start | bytes 262144 | tf_op jit(solution)/shard_map/all_to_all | solution.py:183
  55.2 12.7 %all_gather.7 = bf16[256,256]{0,1:T(8,128)(2,1)S(1)} all-gather(bf16[256,32]{0,1:T(8,128)(2,1)S(1)} %convolution_convert_fusion.11), channel_id=1, replica_groups=mesh['wide'=64,'narrow'=8] {'narrow'}, dimensions={1}, use_global_device_ids=true | all-gather | bytes 147456 | tf_op jit(solution)/shard_map/all_gather | solution.py:121
  71.5 2.2 %broadcast_multiply_fusion = f32[16,16,3,64]{3,2,1,0:T(4,128)} fusion(f32[16,16,3,64]{3,2,1,0:T(4,128)S(1)} %reshape.238, f32[16,16,3]{2,1,0:T(8,128)} %copy.95), kind=kLoop, calls=%fused_computation.72 | loop fusion | flops 49152 | bytes 396288 | tf_op jit(solution)/shard_map/rsh,rshp,rsn->rhpn/dot_general | solution.py:73
  73.7 1.5 divide_multiply_fusion.1
  75.2 12.7 %all-to-all-start.2 = ((bf16[64,3,256]{2,1,0:T(4,128)(2,1)}), bf16[64,3,256]{2,1,0:T(4,128)(2,1)S(1)}, u32[]{:S(2)}, u32[]{:S(2)}) async-start(bf16[64,3,256]{2,1,0:T(4,128)(2,1)} %copy.101), calls=%async_computation.2 | async-start | bytes 262144 | tf_op jit(solution)/shard_map/all_to_all | solution.py:184
  87.9 3.8 %add_convert_fusion = bf16[16,3,64,128]{3,2,1,0:T(8,128)(2,1)S(1)} fusion(bf16[16,3,64,128]{3,2,1,0:T(8,128)(2,1)S(1)} %copy-done.2, f32[16,3]{1,0:T(8,128)S(1)} %copy.93, f32[16,16,3,64]{3,2,1,0:T(4,128)} %broadcast_multiply_fusion, f32[16,16,256]{2,1,0:T(8,128)S(1)} %divide_multiply_fusion.1), kind=kOutput, calls=%fused_computation.21 | convolution fusion | flops 77070336 | bytes 1908736 | tf_op jit(solution)/shard_map/rsh,rshp,rsn->rhpn/dot_general | solution.py:73
  91.7 1.8 fusion.2
  93.5 2.5 %copy.114 = bf16[8,8,192,128]{3,2,1,0:T(8,128)(2,1)} copy(bf16[8,8,192,128]{3,1,2,0:T(8,128)(2,1)S(1)} %fusion.2) | data formatting | bytes 6291456
  96.0 2.8 %all-to-all-done.2 = bf16[64,3,256]{2,1,0:T(4,128)(2,1)S(1)} async-done(((bf16[64,3,256]{2,1,0:T(4,128)(2,1)}), bf16[64,3,256]{2,1,0:T(4,128)(2,1)S(1)}, u32[]{:S(2)}, u32[]{:S(2)}) %all-to-all-start.2) | async-done | bytes 98336 | tf_op jit(solution)/shard_map/all_to_all | solution.py:184
  98.8 10.3 %all-to-all-start = ((bf16[64,3,64,128]{3,2,1,0:T(8,128)(2,1)}), bf16[64,3,64,128]{3,2,1,0:T(8,128)(2,1)}, u32[]{:S(2)}, u32[]{:S(2)}) async-start(bf16[64,3,64,128]{3,2,1,0:T(8,128)(2,1)} %bitcast.87), calls=%async_computation | async-start | bytes 6291456 | tf_op jit(solution)/shard_map/all_to_all | solution.py:182
  111.1 1.7 convolution_multiply_fusion
  115.1 14.5 %psum.14 = f32[256,1]{0,1:T(1,128)S(1)} all-reduce(f32[256,1]{0,1:T(1,128)S(1)} %bitcast.96), channel_id=1, replica_groups=mesh['wide'=64,'narrow'=8] {'narrow'}, use_global_device_ids=true, to_apply=%region_3.4 | all-reduce | flops 256 | bytes 2048 | tf_op jit(solution)/shard_map/psum | solution.py:144
  129.7 2.4 %convolution_convert_fusion.2 = bf16[256,1536]{1,0:T(8,128)(2,1)} fusion(bf16[192,1536]{1,0:T(8,128)(2,1)} %param.40, f32[192]{0:T(256)S(1)} %copy-done.24, f32[256]{0:T(256)S(1)} %bitcast.105, f32[256,192]{1,0:T(8,128)S(1)} %reshape.239, bf16[256,384]{1,0:T(8,128)(2,1)} %copy-done.6), kind=kOutput, calls=%fused_computation.7 | convolution fusion | flops 151830528 | bytes 1705728 | tf_op jit(solution)/shard_map/dot_general | solution.py:148
  132.2 18.0 %reduce-window.6 = s32[64,8,128]{2,1,0:T(8,128)S(1)} reduce-window(s32[64,8,128]{2,1,0:T(8,128)S(1)} %fusion.41, s32[]{:T(128)} %constant.71.clone.1), window={size=1x1x128 pad=0_0x0_0x127_0}, to_apply=%region_6.7 | reduce-window | flops 8323072 | bytes 524292 | tf_op jit(solution)/shard_map/reduce-window
  150.8 4.5 %gather_fusion.1 = s32[1024]{0:T(1024)S(1)} fusion(s32[1024]{0:T(1024)S(1)} %fusion.37, s32[1024]{0:T(1024)S(1)} %fusion.81), kind=kCustom, calls=%fused_computation.clone | custom fusion | bytes 12288 | tf_op jit(solution)/shard_map/jit(_take)/gather | solution.py:163
  156.2 1.7 convolution_convert_fusion.10
  158.6 45.9 %all-reduce.3.cloned.1.call-done = bf16[256,1536]{1,0:T(8,128)(2,1)} async-done(((bf16[256,1536]{1,0:T(8,128)(2,1)}), bf16[256,1536]{1,0:T(8,128)(2,1)}) %all-reduce.3.cloned.1.call-update) | async-done | bytes 786448 | tf_op jit(solution)/shard_map/psum | solution.py:149
  204.5 1.5 fusion.3
  206.8 1.3 convolution_convert_fusion.3
  208.2 3.7 %fusion.10 = bf16[2,8,192,128]{3,1,2,0:T(8,128)(2,1)S(1)} fusion(bf16[16,64]{1,0:T(8,128)(2,1)S(1)} %convolution_convert_fusion.12, bf16[8,8,192,128]{3,2,1,0:T(8,128)(2,1)} %bitcast.34), kind=kOutput, calls=%fused_computation.22 | convolution fusion | flops 50724864 | bytes 3934208 | tf_op jit(solution)/shard_map/dot_general | solution.py:198
  (125 shorter events, 21.5 us)
Async XLA Ops:
  7.2 199.7 %copy-start = (bf16[1536,403]{0,1:T(8,128)(2,1)S(1)}, bf16[1536,403]{0,1:T(8,128)(2,1)}, u32[]{:S(2)}) copy-start(bf16[1536,403]{0,1:T(8,128)(2,1)} %param.42) | copy-start | bytes 3714052
  7.2 3.7 %copy-start.1 = (s32[1024]{0:T(1024)S(1)}, s32[1024]{0:T(1024)}, u32[]{:S(2)}) copy-start(s32[1024]{0:T(1024)} %param.45) | copy-start | bytes 12292
  10.9 4.6 %copy-start.12 = (s32[1024]{0:T(1024)S(1)}, s32[1024]{0:T(1024)}, u32[]{:S(2)}) copy-start(s32[1024]{0:T(1024)} %param.43) | copy-start | bytes 12292
  10.9 5.3 %copy-start.10 = (bf16[16,3,192]{2,0,1:T(8,128)(2,1)S(1)}, bf16[16,3,192]{2,0,1:T(8,128)(2,1)}, u32[]{:S(2)}) copy-start(bf16[16,3,192]{2,0,1:T(8,128)(2,1)} %param.26) | copy-start | bytes 55300
  10.9 5.3 %copy-start.7 = (bf16[256,192]{0,1:T(8,128)(2,1)S(1)}, bf16[256,192]{0,1:T(8,128)(2,1)}, u32[]{:S(2)}) copy-start(bf16[256,192]{0,1:T(8,128)(2,1)} %param.24) | copy-start | bytes 294916
  16.1 52.2 %copy-start.15 = (s32[16]{0:T(128)}, s32[16]{0:T(128)S(1)}, u32[]{:S(2)}) copy-start(s32[16]{0:T(128)S(1)} %dynamic_slice.10) | copy-start | bytes 196
  16.2 14.3 %copy-start.22 = (f32[1536]{0:T(1024)S(1)}, f32[1536]{0:T(1024)}, u32[]{:S(2)}) copy-start(f32[1536]{0:T(1024)} %param.28) | copy-start | bytes 18436
  30.5 20.7 %copy-start.25 = (f32[3]{0:T(128)S(1)}, f32[3]{0:T(128)}, u32[]{:S(2)}) copy-start(f32[3]{0:T(128)} %param.33) | copy-start | bytes 40
  30.5 20.7 %copy-start.13 = (bf16[4,192]{1,0:T(4,128)(2,1)S(1)}, bf16[4,192]{1,0:T(4,128)(2,1)}, u32[]{:S(2)}) copy-start(bf16[4,192]{1,0:T(4,128)(2,1)} %param.34) | copy-start | bytes 4612
  30.5 20.7 %copy-start.14 = (bf16[4,256]{1,0:T(4,128)(2,1)S(1)}, bf16[4,256]{1,0:T(4,128)(2,1)}, u32[]{:S(2)}) copy-start(bf16[4,256]{1,0:T(4,128)(2,1)} %param.36) | copy-start | bytes 6148
  30.5 21.4 %copy-start.11 = (bf16[16,3,256]{2,0,1:T(8,128)(2,1)S(1)}, bf16[16,3,256]{2,0,1:T(8,128)(2,1)}, u32[]{:S(2)}) copy-start(bf16[16,3,256]{2,0,1:T(8,128)(2,1)} %param.27) | copy-start | bytes 73732
  30.5 21.4 %copy-start.21 = (bf16[1536,3]{0,1:T(4,128)(2,1)S(1)}, bf16[1536,3]{0,1:T(4,128)(2,1)}, u32[]{:S(2)}) copy-start(bf16[1536,3]{0,1:T(4,128)(2,1)} %param.31) | copy-start | bytes 27652
  32.5 19.8 %copy-start.20 = (bf16[1536,32]{0,1:T(8,128)(2,1)S(1)}, bf16[1536,32]{0,1:T(8,128)(2,1)}, u32[]{:S(2)}) copy-start(bf16[1536,32]{0,1:T(8,128)(2,1)} %param.30) | copy-start | bytes 294916
  34.4 40.8 %all-to-all-start.1 = ((bf16[64,3,192]{2,1,0:T(4,128)(2,1)}), bf16[64,3,192]{2,1,0:T(4,128)(2,1)}, u32[]{:S(2)}, u32[]{:S(2)}) async-start(bf16[64,3,192]{2,1,0:T(4,128)(2,1)} %copy.98), calls=%async_computation.1 | async-start | bytes 262144 | tf_op jit(solution)/shard_map/all_to_all | solution.py:183
  52.3 17.1 %copy-start.17 = (f32[192]{0:T(256)S(1)}, f32[192]{0:T(256)}, u32[]{:S(2)}) copy-start(f32[192]{0:T(256)} %param.35) | copy-start | bytes 2308
  69.4 18.5 %copy-start.2 = (bf16[16,3,64,128]{3,2,1,0:T(8,128)(2,1)S(1)}, bf16[16,3,64,128]{3,2,1,0:T(8,128)(2,1)}, u32[]{:S(2)}) copy-start(bf16[16,3,64,128]{3,2,1,0:T(8,128)(2,1)} %param.25) | copy-start | bytes 2359300
  75.2 23.6 %all-to-all-start.2 = ((bf16[64,3,256]{2,1,0:T(4,128)(2,1)}), bf16[64,3,256]{2,1,0:T(4,128)(2,1)S(1)}, u32[]{:S(2)}, u32[]{:S(2)}) async-start(bf16[64,3,256]{2,1,0:T(4,128)(2,1)} %copy.101), calls=%async_computation.2 | async-start | bytes 262144 | tf_op jit(solution)/shard_map/all_to_all | solution.py:184
  98.8 109.4 %all-to-all-start = ((bf16[64,3,64,128]{3,2,1,0:T(8,128)(2,1)}), bf16[64,3,64,128]{3,2,1,0:T(8,128)(2,1)}, u32[]{:S(2)}, u32[]{:S(2)}) async-start(bf16[64,3,64,128]{3,2,1,0:T(8,128)(2,1)} %bitcast.87), calls=%async_computation | async-start | bytes 6291456 | tf_op jit(solution)/shard_map/all_to_all | solution.py:182
  109.0 3.8 %copy-start.26 = (f32[3]{0:T(128)S(1)}, f32[3]{0:T(128)}, u32[]{:S(2)}) copy-start(f32[3]{0:T(128)} %param.38) | copy-start | bytes 40
  109.1 95.4 %all-reduce.3.cloned.1.call-start = ((), (), s32[]{:S(2)}) async-start(), calls=%async_computation.3 | async-start | bytes 1572864 | tf_op jit(solution)/shard_map/psum | solution.py:149
  112.9 16.8 %copy-start.24 = (f32[192]{0:T(256)S(1)}, f32[192]{0:T(256)}, u32[]{:S(2)}) copy-start(f32[192]{0:T(256)} %param.39) | copy-start | bytes 2308
  150.8 4.6 %copy-start.16 = (pred[1024]{0:T(1024)(128)(4,1)S(1)}, pred[1024]{0:T(1024)(128)(4,1)}, u32[]{:S(2)}) copy-start(pred[1024]{0:T(1024)(128)(4,1)} %get-tuple-element.28) | copy-start | bytes 3076
  150.8 4.6 %copy-start.18 = (pred[1024]{0:T(1024)(128)(4,1)S(1)}, pred[1024]{0:T(1024)(128)(4,1)}, u32[]{:S(2)}) copy-start(pred[1024]{0:T(1024)(128)(4,1)} %get-tuple-element.26) | copy-start | bytes 3076
  156.2 50.7 %copy-start.23 = (f32[1536]{0:T(1024)S(1)}, f32[1536]{0:T(1024)}, u32[]{:S(2)}) copy-start(f32[1536]{0:T(1024)} %param.41) | copy-start | bytes 18436
  (7 other events, 11.7 us)
Sparse Core Ops, SparseCore 0:
  132.2 72.1 all-reduce.2
where the time goes:
time: 220 us
  waiting for transfers between devices  48.7 us (22%)
  blocking collectives  41 us (19%)
  starting transfers between devices  39.6 us (18%)
  other arithmetic  30.4 us (14%)
  local copies, waits for them, and re-layouts  22.8 us (10%)
  matrix products  22.6 us (10%)
  between operations  14.6 us (7%)
    psum x1, waiting for transfers between devices, local(): lax.psum(partial_sum.astype(jnp.bfloat16), 'narrow').astype(jnp.float32)  45.9 us
    another operation x3, other arithmetic  18.2 us
    all_to_all x1, starting transfers between devices, local(): lax.all_to_all(inner_bucket, 'wide', split_axis=0, concat_axis=0, tiled=T...  16.6 us
    psum x1, blocking collectives, local(): squares = lax.psum(jnp.sum(gated * gated, axis=1, keepdims=True), 'narrow')  14.5 us
    all_gather x1, blocking collectives, local(): full_rows = lax.all_gather(hidden, 'narrow', axis=1, tiled=True)  13.7 us
    all_gather x1, blocking collectives, local(): shared_in = lax.all_gather(shared_piece, 'narrow', axis=1, tiled=True)  12.7 us
    all_to_all x1, starting transfers between devices, local(): lax.all_to_all(shared_bucket, 'wide', split_axis=0, concat_axis=0, tiled=...  12.7 us
    all_to_all x1, starting transfers between devices, local(): lax.all_to_all(state_bucket, 'wide', split_axis=0, concat_axis=0, tiled=T...  10.3 us
  transfers between devices with their start and end apart: 4, of which 2 were waited for; matrix products, arithmetic and copies ran while one was open for 26% of the time, Pallas kernels for 0%

commit v1 on v0

--- a/solution.py
+++ b/solution.py
@@ -146,7 +146,9 @@
         gated * lax.rsqrt(squares / (block * narrow_count) + EPSILON) * gated_gain
     ).astype(jnp.bfloat16)
     partial_sum = jnp.dot(gated_norm, w_output, preferred_element_type=jnp.float32)
-    whole_sum = lax.psum(partial_sum.astype(jnp.bfloat16), "narrow").astype(jnp.float32)
+    whole_sum = jnp.sum(lax.all_gather(partial_sum.astype(jnp.bfloat16), "narrow"), axis=0).astype(
+        jnp.float32
+    )
     new_full = (full_rows.astype(jnp.float32) + whole_sum).astype(jnp.bfloat16)
     new_part = lax.dynamic_slice_in_dim(
         new_full, lax.axis_index("narrow") * hidden.shape[1], hidden.shape[1], 1

time: 220 us -> 272 us (1.24)
  the two profiles are of different devices: /device:TPU:24 before, /device:TPU:46 now
where the time goes in v1:
time: 272 us; the launch traced here: 271 us
  waiting for transfers between devices  79.9 us (29%)
  starting transfers between devices  39.9 us (15%)
  blocking collectives  37.4 us (14%)
  other arithmetic  36.2 us (13%)
  local copies, waits for them, and re-layouts  35.6 us (13%)
  matrix products  27.1 us (10%)
  between operations  14.5 us (5%)
    all_to_all x1, waiting for transfers between devices, local(): lax.all_to_all(state_bucket, 'wide', split_axis=0, concat_axis=0, tiled=T...  77.9 us
    another operation x3, other arithmetic  18.2 us
    all_to_all x1, starting transfers between devices, local(): lax.all_to_all(inner_bucket, 'wide', split_axis=0, concat_axis=0, tiled=T...  16.3 us
    all_gather x1, blocking collectives, local(): full_rows = lax.all_gather(hidden, 'narrow', axis=1, tiled=True)  13.8 us
    all_to_all x1, starting transfers between devices, local(): lax.all_to_all(shared_bucket, 'wide', split_axis=0, concat_axis=0, tiled=...  12.7 us
    all_gather x1, blocking collectives, local(): shared_in = lax.all_gather(shared_piece, 'narrow', axis=1, tiled=True)  12.7 us
    psum x1, blocking collectives, local(): squares = lax.psum(jnp.sum(gated * gated, axis=1, keepdims=True), 'narrow')  10.9 us
    all_to_all x1, starting transfers between devices, local(): lax.all_to_all(state_bucket, 'wide', split_axis=0, concat_axis=0, tiled=T...  10.9 us
  transfers between devices with their start and end apart: 4, of which 2 were waited for; matrix products, arithmetic and copies ran while one was open for 25% of the time, Pallas kernels for 0%

profile of v1, /device:TPU:46, one launch (start us, length us, event | category | flops | bytes accessed | tf_op | source)
XLA Modules:
  0.0 270.8 jit_solution(4678848121935566070)
XLA Ops:
  8.5 13.8 %all_gather.12 = bf16[256,1536]{0,1:T(8,128)(2,1)S(1)} all-gather(bf16[256,192]{0,1:T(8,128)(2,1)} %param.24), channel_id=1, replica_groups=mesh['wide'=64,'narrow'=8] {'narrow'}, dimensions={1}, use_global_device_ids=true | all-gather | bytes 884736 | tf_op jit(solution)/shard_map/all_gather | solution.py:106
  28.2 12.7 %all_gather.13 = bf16[256,256]{0,1:T(8,128)(2,1)S(1)} all-gather(bf16[256,32]{0,1:T(8,128)(2,1)S(1)} %convolution_convert_fusion.11), channel_id=1, replica_groups=mesh['wide'=64,'narrow'=8] {'narrow'}, dimensions={1}, use_global_device_ids=true | all-gather | bytes 147456 | tf_op jit(solution)/shard_map/all_gather | solution.py:121
  42.7 2.0 convolution_convert_fusion.4
  46.7 2.5 convolution_multiply_fusion
  49.2 2.0 fusion.14
  54.6 10.9 %psum.7 = f32[256,1]{0,1:T(1,128)S(1)} all-reduce(f32[256,1]{0,1:T(1,128)S(1)} %bitcast.98), channel_id=1, replica_groups=mesh['wide'=64,'narrow'=8] {'narrow'}, use_global_device_ids=true, to_apply=%region_3.4 | all-reduce | flops 256 | bytes 2048 | tf_op jit(solution)/shard_map/psum | solution.py:144
  65.6 2.5 convolution_convert_fusion.2
  68.2 8.8 %gather_fusion.2 = s32[1024]{0:T(1024)} fusion(s32[1024]{0:T(1024)S(1)} %copy-done.1, s32[1024]{0:T(1024)S(1)} %fusion.81), kind=kCustom, calls=%fused_computation.1.clone | custom fusion | bytes 12288 | tf_op jit(solution)/shard_map/jit(_take)/gather | solution.py:164
  84.9 16.3 %all-to-all-start.1 = ((bf16[64,3,192]{2,1,0:T(4,128)(2,1)}), bf16[64,3,192]{2,1,0:T(4,128)(2,1)S(1)}, u32[]{:S(2)}, u32[]{:S(2)}) async-start(bf16[64,3,192]{2,1,0:T(4,128)(2,1)} %copy.117), calls=%async_computation.1 | async-start | bytes 262144 | tf_op jit(solution)/shard_map/all_to_all | solution.py:185
  102.6 1.4 copy.127
  104.0 1.4 multiply_reduce_fusion.1
  107.5 1.4 select_multiply_fusion
  111.9 2.2 broadcast_multiply_fusion
  114.0 12.7 %all-to-all-start.2 = ((bf16[64,3,256]{2,1,0:T(4,128)(2,1)}), bf16[64,3,256]{2,1,0:T(4,128)(2,1)S(1)}, u32[]{:S(2)}, u32[]{:S(2)}) async-start(bf16[64,3,256]{2,1,0:T(4,128)(2,1)} %copy.120), calls=%async_computation.2 | async-start | bytes 262144 | tf_op jit(solution)/shard_map/all_to_all | solution.py:186
  126.8 3.8 %add_convert_fusion = bf16[16,3,64,128]{3,2,1,0:T(8,128)(2,1)S(1)} fusion(bf16[16,3,64,128]{3,2,1,0:T(8,128)(2,1)S(1)} %copy-done.3, f32[16,3]{1,0:T(8,128)S(1)} %copy-done.11, f32[16,16,3,64]{3,2,1,0:T(4,128)} %broadcast_multiply_fusion, f32[16,16,256]{2,1,0:T(8,128)S(1)} %divide_multiply_fusion.1), kind=kOutput, calls=%fused_computation.21 | convolution fusion | flops 77070336 | bytes 1908736 | tf_op jit(solution)/shard_map/rsh,rshp,rsn->rhpn/dot_general | solution.py:73
  131.7 2.6 copy.133
  134.3 2.0 all-to-all-done.2
  136.3 10.9 %all-to-all-start = ((bf16[64,3,64,128]{3,2,1,0:T(8,128)(2,1)}), bf16[64,3,64,128]{3,2,1,0:T(8,128)(2,1)}, u32[]{:S(2)}, u32[]{:S(2)}) async-start(bf16[64,3,64,128]{3,2,1,0:T(8,128)(2,1)} %bitcast.88), calls=%async_computation | async-start | bytes 6291456 | tf_op jit(solution)/shard_map/all_to_all | solution.py:184
  147.2 18.0 %reduce-window.6 = s32[64,8,128]{2,1,0:T(8,128)S(1)} reduce-window(s32[64,8,128]{2,1,0:T(8,128)S(1)} %fusion.41, s32[]{:T(128)} %constant.73.clone.1), window={size=1x1x128 pad=0_0x0_0x127_0}, to_apply=%region_6.7 | reduce-window | flops 8323072 | bytes 524292 | tf_op jit(solution)/shard_map/reduce-window
  165.8 4.5 %gather_fusion.1 = s32[1024]{0:T(1024)S(1)} fusion(s32[1024]{0:T(1024)S(1)} %fusion.37, s32[1024]{0:T(1024)S(1)} %fusion.81), kind=kCustom, calls=%fused_computation.clone | custom fusion | bytes 12288 | tf_op jit(solution)/shard_map/jit(_take)/gather | solution.py:165
  172.7 77.9 %all-to-all-done = bf16[64,3,64,128]{3,2,1,0:T(8,128)(2,1)} async-done(((bf16[64,3,64,128]{3,2,1,0:T(8,128)(2,1)}), bf16[64,3,64,128]{3,2,1,0:T(8,128)(2,1)}, u32[]{:S(2)}, u32[]{:S(2)}) %all-to-all-start) | async-done | bytes 3145760 | tf_op jit(solution)/shard_map/all_to_all | solution.py:184
  250.6 3.7 %fusion.10 = bf16[2,8,192,128]{3,1,2,0:T(8,128)(2,1)S(1)} fusion(bf16[16,64]{1,0:T(8,128)(2,1)S(1)} %convolution_convert_fusion.12, bf16[8,8,192,128]{3,2,1,0:T(8,128)(2,1)} %bitcast.35), kind=kOutput, calls=%fused_computation.22 | convolution fusion | flops 50724864 | bytes 3934208 | tf_op jit(solution)/shard_map/dot_general | solution.py:200
  255.3 4.1 %reduce_sum.50 = bf16[256,1536]{1,0:T(8,128)(2,1)S(1)} reduce(bf16[8,256,1536]{2,1,0:T(8,128)(2,1)} %bitcast.89, bf16[]{:T(256)} %constant.72.clone.1), dimensions={0}, to_apply=%region_4.5 | reduce | flops 2752512 | bytes 7077890 | tf_op jit(solution)/shard_map/reduce_sum | solution.py:149
  261.5 2.4 convolution_convert_fusion.3
  (132 shorter events, 35.7 us)
Async XLA Ops:
  7.2 254.4 %copy-start = (bf16[1536,403]{0,1:T(8,128)(2,1)S(1)}, bf16[1536,403]{0,1:T(8,128)(2,1)}, u32[]{:S(2)}) copy-start(bf16[1536,403]{0,1:T(8,128)(2,1)} %param.42) | copy-start | bytes 3714052
  7.2 248.1 %all-gather.3.cloned.1.call-start = ((), (), s32[]{:S(2)}) async-start(), calls=%async_computation.3 | async-start | bytes 7077888 | tf_op jit(solution)/shard_map/all_gather | solution.py:149
  8.5 14.4 %copy-start.27 = (bf16[1536,3]{0,1:T(4,128)(2,1)S(1)}, bf16[1536,3]{0,1:T(4,128)(2,1)}, u32[]{:S(2)}) copy-start(bf16[1536,3]{0,1:T(4,128)(2,1)} %param.31) | copy-start | bytes 27652
  8.5 14.4 %copy-start.28 = (f32[1536]{0:T(1024)S(1)}, f32[1536]{0:T(1024)}, u32[]{:S(2)}) copy-start(f32[1536]{0:T(1024)} %param.28) | copy-start | bytes 18436
  22.6 3.1 %copy-start.18 = (bf16[4,256]{1,0:T(4,128)(2,1)S(1)}, bf16[4,256]{1,0:T(4,128)(2,1)}, u32[]{:S(2)}) copy-start(bf16[4,256]{1,0:T(4,128)(2,1)} %param.36) | copy-start | bytes 6148
  22.6 3.1 %copy-start.12 = (bf16[16,3,192]{2,0,1:T(8,128)(2,1)S(1)}, bf16[16,3,192]{2,0,1:T(8,128)(2,1)}, u32[]{:S(2)}) copy-start(bf16[16,3,192]{2,0,1:T(8,128)(2,1)} %param.26) | copy-start | bytes 55300
  22.6 3.8 %copy-start.13 = (bf16[16,3,256]{2,0,1:T(8,128)(2,1)S(1)}, bf16[16,3,256]{2,0,1:T(8,128)(2,1)}, u32[]{:S(2)}) copy-start(bf16[16,3,256]{2,0,1:T(8,128)(2,1)} %param.27) | copy-start | bytes 73732
  22.6 3.8 %copy-start.26 = (bf16[1536,32]{0,1:T(8,128)(2,1)S(1)}, bf16[1536,32]{0,1:T(8,128)(2,1)}, u32[]{:S(2)}) copy-start(bf16[1536,32]{0,1:T(8,128)(2,1)} %param.30) | copy-start | bytes 294916
  23.5 17.6 %copy-start.22 = (f32[256]{0:T(256)S(1)}, f32[256]{0:T(256)}, u32[]{:S(2)}) copy-start(f32[256]{0:T(256)} %param.37) | copy-start | bytes 3076
  42.7 2.8 %copy-start.23 = (f32[192]{0:T(256)S(1)}, f32[192]{0:T(256)}, u32[]{:S(2)}) copy-start(f32[192]{0:T(256)} %param.35) | copy-start | bytes 2308
  42.7 4.0 %copy-start.3 = (bf16[16,3,64,128]{3,2,1,0:T(8,128)(2,1)S(1)}, bf16[16,3,64,128]{3,2,1,0:T(8,128)(2,1)}, u32[]{:S(2)}) copy-start(bf16[16,3,64,128]{3,2,1,0:T(8,128)(2,1)} %param.25) | copy-start | bytes 2359300
  54.6 13.5 %copy-start.14 = (s32[1024]{0:T(1024)S(1)}, s32[1024]{0:T(1024)}, u32[]{:S(2)}) copy-start(s32[1024]{0:T(1024)} %param.43) | copy-start | bytes 12292
  54.6 13.5 %copy-start.1 = (s32[1024]{0:T(1024)S(1)}, s32[1024]{0:T(1024)}, u32[]{:S(2)}) copy-start(s32[1024]{0:T(1024)} %param.45) | copy-start | bytes 12292
  68.2 11.4 %copy-start.2 = (s32[1024]{0:T(1024)S(1)}, s32[1024]{0:T(1024)}, u32[]{:S(2)}) copy-start(s32[1024]{0:T(1024)} %param.44) | copy-start | bytes 12292
  68.2 14.1 %copy-start.8 = (bf16[256,192]{1,0:T(8,128)(2,1)S(1)}, bf16[256,192]{1,0:T(8,128)(2,1)}, u32[]{:S(2)}) copy-start(bf16[256,192]{1,0:T(8,128)(2,1)} %copy-done.7) | copy-start | bytes 294916
  77.0 32.9 %copy-start.6 = (bf16[256,256]{1,0:T(8,128)(2,1)S(1)}, bf16[256,256]{1,0:T(8,128)(2,1)}, u32[]{:S(2)}) copy-start(bf16[256,256]{1,0:T(8,128)(2,1)} %copy-done.5) | copy-start | bytes 393220
  81.6 22.4 %copy-start.15 = (s32[16]{0:T(128)}, s32[16]{0:T(128)S(1)}, u32[]{:S(2)}) copy-start(s32[16]{0:T(128)S(1)} %and_select_fusion) | copy-start | bytes 196
  81.6 29.2 %copy-start.19 = (s32[16]{0:T(128)S(1)}, s32[16]{0:T(128)}, u32[]{:S(2)}) copy-start(s32[16]{0:T(128)} %dynamic_slice.10) | copy-start | bytes 196
  84.9 29.2 %all-to-all-start.1 = ((bf16[64,3,192]{2,1,0:T(4,128)(2,1)}), bf16[64,3,192]{2,1,0:T(4,128)(2,1)S(1)}, u32[]{:S(2)}, u32[]{:S(2)}) async-start(bf16[64,3,192]{2,1,0:T(4,128)(2,1)} %copy.117), calls=%async_computation.1 | async-start | bytes 262144 | tf_op jit(solution)/shard_map/all_to_all | solution.py:185
  109.0 17.8 %copy-start.11 = (f32[16,3]{1,0:T(8,128)S(1)}, f32[16,3]{1,0:T(8,128)}, u32[]{:S(2)}) copy-start(f32[16,3]{1,0:T(8,128)} %copy.112) | copy-start | bytes 580
  114.0 22.2 %all-to-all-start.2 = ((bf16[64,3,256]{2,1,0:T(4,128)(2,1)}), bf16[64,3,256]{2,1,0:T(4,128)(2,1)S(1)}, u32[]{:S(2)}, u32[]{:S(2)}) async-start(bf16[64,3,256]{2,1,0:T(4,128)(2,1)} %copy.120), calls=%async_computation.2 | async-start | bytes 262144 | tf_op jit(solution)/shard_map/all_to_all | solution.py:186
  136.3 114.3 %all-to-all-start = ((bf16[64,3,64,128]{3,2,1,0:T(8,128)(2,1)}), bf16[64,3,64,128]{3,2,1,0:T(8,128)(2,1)}, u32[]{:S(2)}, u32[]{:S(2)}) async-start(bf16[64,3,64,128]{3,2,1,0:T(8,128)(2,1)} %bitcast.88), calls=%async_computation | async-start | bytes 6291456 | tf_op jit(solution)/shard_map/all_to_all | solution.py:184
  165.8 4.6 %copy-start.21 = (pred[1024]{0:T(1024)(128)(4,1)S(1)}, pred[1024]{0:T(1024)(128)(4,1)}, u32[]{:S(2)}) copy-start(pred[1024]{0:T(1024)(128)(4,1)} %get-tuple-element.23) | copy-start | bytes 3076
  165.8 4.6 %copy-start.24 = (pred[1024]{0:T(1024)(128)(4,1)S(1)}, pred[1024]{0:T(1024)(128)(4,1)}, u32[]{:S(2)}) copy-start(pred[1024]{0:T(1024)(128)(4,1)} %get-tuple-element.21) | copy-start | bytes 3076
  (10 other events, 14.8 us)
Sparse Core Ops, SparseCore 0:
  68.2 50.2 all-gather.2
